TPU v7x, 32 devices: a whole 2x2x4 slice. The times are simulated.
32 devices in a mesh: groups: 2 (over y), seq: 16 (over z, x, core).
Axes of the slice: x: 2, y: 2, z: 4, core: 2. Of those that a mesh axis runs over, the one named last changes fastest.
Arguments:
- span_frames: bfloat16 [512, 512], P(('groups', 'seq')), parts along dimension 0, may hold values from -3 to 3
- query_rows: bfloat16 [512, 512], P(('groups', 'seq')), parts along dimension 0, may hold values from -12 to 12
- key_rows: bfloat16 [16384, 512], P(('groups', 'seq')), parts along dimension 0, may hold values from -6 to 6
- context_frames: bfloat16 [16384, 512], P(('groups', 'seq')), parts along dimension 0, may hold values from -6 to 6
- key_mask: int32 [16384], P(('groups', 'seq')), parts along dimension 0, may hold values from 0 to 1, as said below
- value_weight: bfloat16 [512, 512], replicated, may hold values from -0.5 to 0.5
- out_weight: bfloat16 [512, 512], replicated, may hold values from -0.25 to 0.25
- expand_weight: bfloat16 [512, 1024], replicated, may hold values from -0.25 to 0.25
- depth_weight: float32 [31, 512], replicated, may hold values from -1 to 1
- norm_scale: float32 [512], replicated, may hold values from 0.5 to 2
- norm_shift: float32 [512], replicated, may hold values from -3 to 3
- project_weight: bfloat16 [512, 512], replicated, may hold values from -0.25 to 0.25
Outputs:
- layer_out: bfloat16 [512, 512], P(('groups', 'seq')), parts along dimension 0
There are 2 independent parts, one for each index of `groups`. A program takes and returns all parts, laid end to end along the dimension named above; an argument that names none is the same for every part. Nothing has to cross between parts.
Inputs may be any that keep to these rules, and one draw needn't show every extreme that they name: `key_mask`: within each block of 512 frames held by one index of seq, the real frames come first and there is at least one.
All inputs are finite; a program needn't handle non-finite values.
Results may differ from a plain program's by a relative error of at most 0.013.
Values may be sent and summed in bfloat16 or wider, within the bound.
A program may use at most 384 MiB of HBM per device.

v0:
```python
import math

import jax
import jax.numpy as jnp
from jax import lax
from jax.sharding import PartitionSpec as P

HEADS = 8


def combined_all(value, axis, join):
    pieces = jax.tree.map(lambda part: lax.all_gather(part, axis), value)
    head = jax.tree.map(lambda part: part[0], pieces)
    tail = jax.tree.map(lambda part: part[1:], pieces)
    so_far, _ = lax.scan(lambda so_far, section: (join(so_far, section), None), head, tail)
    return so_far


def with_halo(block, sides, width):
    for axis, dim in sides:
        count = lax.axis_size(axis)
        forward = [(i, i + 1) for i in range(count - 1)]
        backward = [(target, source) for source, target in forward]
        low = lax.ppermute(
            lax.slice_in_dim(block, block.shape[dim] - width, None, axis=dim), axis, forward
        )
        high = lax.ppermute(lax.slice_in_dim(block, 0, width, axis=dim), axis, backward)
        block = jnp.concatenate([low, block, high], axis=dim)
    return block


def combine_partial(first_part, second_part):
    out_first, lse_first = first_part
    out_second, lse_second = second_part
    width = out_first.shape[1] // lse_first.shape[0]
    joint = jnp.logaddexp(lse_first, lse_second)
    share_first = jnp.repeat(jnp.exp(lse_first - joint).T, width, axis=1)
    share_second = jnp.repeat(jnp.exp(lse_second - joint).T, width, axis=1)
    return (out_first * share_first + out_second * share_second, joint)


def body(
    span_frames,
    query_rows,
    key_rows,
    context_frames,
    key_mask,
    value_weight,
    out_weight,
    expand_weight,
    depth_weight,
    norm_scale,
    norm_shift,
    project_weight,
):
    width = key_rows.shape[1]
    head_dim = width // HEADS
    scale = 1.0 / math.sqrt(head_dim)
    values = jnp.dot(context_frames, value_weight, preferred_element_type=jnp.float32).astype(
        jnp.bfloat16
    )
    key_heads = key_rows.reshape(key_rows.shape[0], HEADS, head_dim)
    value_heads = values.reshape(values.shape[0], HEADS, head_dim)
    valid = key_mask > 0
    gathered = lax.all_gather(query_rows, "seq", axis=0, tiled=True)
    own_rows = query_rows.shape[0]
    total_rows = gathered.shape[0]
    block = min(512, total_rows)
    blocks = total_rows // block
    query_blocks = gathered.reshape(blocks, block, HEADS, head_dim)

    def block_scores(query_block):
        scores = (
            jnp.einsum("bhd,khd->hbk", query_block, key_heads, preferred_element_type=jnp.float32)
            * scale
        )
        return jnp.where(valid[None, None, :], scores, -1e30)

    def weighted(scores, shift_rows):
        weights = jnp.exp(scores - shift_rows[:, :, None])
        total = jnp.sum(weights, axis=2)
        numer = jnp.einsum(
            "hbk,khd->bhd",
            weights.astype(jnp.bfloat16),
            value_heads,
            preferred_element_type=jnp.float32,
        )
        return (numer.reshape(numer.shape[0], width), total)

    def merged_block(query_block):
        scores = block_scores(query_block)
        top = jnp.max(scores, axis=2)
        numer, total = weighted(scores, top)
        partial_value = numer / jnp.repeat(total.T, head_dim, axis=1)
        partial_lse = top + jnp.log(total)
        return combined_all((partial_value, partial_lse), "seq", combine_partial)

    merged, merged_lse = lax.map(merged_block, query_blocks)
    merged = merged.reshape(total_rows, width)
    first_row = lax.axis_index("seq") * own_rows
    attended = lax.dynamic_slice_in_dim(merged, first_row, own_rows, 0).astype(jnp.bfloat16)
    wide = span_frames.astype(jnp.float32) + jnp.dot(
        attended, out_weight, preferred_element_type=jnp.float32
    )
    mixed = wide.astype(jnp.bfloat16)
    stream = mixed.astype(jnp.float32)
    centre = jnp.mean(stream, axis=1, keepdims=True)
    spread = jnp.mean((stream - centre) ** 2, axis=1, keepdims=True)
    normed = ((stream - centre) / jnp.sqrt(spread + 1e-05)).astype(jnp.bfloat16)
    expanded = jnp.dot(normed, expand_weight, preferred_element_type=jnp.float32)
    gated = (expanded[:, :width] * jax.nn.sigmoid(expanded[:, width:])).astype(jnp.bfloat16)
    reach = depth_weight.shape[0] // 2
    padded = with_halo(gated, (("seq", 0),), reach).astype(jnp.float32)
    conv = jnp.zeros((own_rows, width), jnp.float32)
    for offset in range(depth_weight.shape[0]):
        conv = conv + padded[offset : offset + own_rows] * depth_weight[offset][None, :]
    normal_conv = conv * norm_scale[None, :] + norm_shift[None, :]
    activated = (normal_conv * jax.nn.sigmoid(normal_conv)).astype(jnp.bfloat16)
    return (stream + jnp.dot(activated, project_weight, preferred_element_type=jnp.float32)).astype(
        jnp.bfloat16
    )


def solution(mesh):
    in_specs = (
        P(("groups", "seq"), None),
        P(("groups", "seq"), None),
        P(("groups", "seq"), None),
        P(("groups", "seq"), None),
        P(("groups", "seq")),
        P(),
        P(),
        P(),
        P(),
        P(),
        P(),
        P(),
    )
    out_specs = P(("groups", "seq"), None)
    return jax.shard_map(body, mesh=mesh, in_specs=in_specs, out_specs=out_specs, check_vma=False)
```

profile of v0, /device:TPU:1, one launch (start us, length us, event | category | flops | bytes accessed | tf_op | source)
XLA Modules:
  0.0 159.2 jit_solution(10683933736203446552)
XLA Ops:
  6.5 0.8 broadcast_compare_fusion
  7.3 23.9 %all_gather.15 = bf16[256,512]{1,0:T(8,128)(2,1)S(1)} all-gather(bf16[16,512]{1,0:T(8,128)(2,1)} %param.15), channel_id=1, replica_groups=mesh['groups'=2,'seq'=16] {'seq'}, dimensions={0}, use_global_device_ids=true | all-gather | bytes 278528 | tf_op jit(solution)/shard_map/all_gather | solution.py:65
  31.3 1.3 copy.21
  32.6 0.8 fusion.5
  33.5 1.2 fusion.6
  34.7 0.5 convolution_convert_fusion
  35.2 1.1 fusion.17
  36.3 1.0 copy.22
  37.4 18.5 %all-gather = f32[128,256]{1,0:T(8,128)S(1)} all-gather(f32[8,256]{1,0:T(8,128)S(1)} %log_add_fusion), channel_id=2, replica_groups=mesh['groups'=2,'seq'=16] {'seq'}, dimensions={0}, use_global_device_ids=true | all-gather | bytes 139264 | tf_op jit(solution)/shard_map/while/body/eval_jaxpr/all_gather | solution.py:12
  55.9 53.4 %all-gather.3.cloned.1.call-done = f32[16,256,512]{2,1,0:T(8,128)} async-done(((f32[1,256,512]{2,1,0:T(8,128)}), f32[16,256,512]{2,1,0:T(8,128)}) %all-gather.3.cloned.1.call-update) | async-done | bytes 8388624 | tf_op jit(solution)/shard_map/while/body/eval_jaxpr/all_gather | solution.py:12
  109.4 1.1 slice_bitcast_fusion
  110.6 7.6 %slice.289 = f32[15,256,512]{2,1,0:T(8,128)} slice(f32[16,256,512]{2,1,0:T(8,128)} %all-gather.3.cloned.1.call-done), slice={[1:16], [0:256], [0:512]} | slice | bytes 15728640 | tf_op jit(solution)/shard_map/while/body/eval_jaxpr/slice | solution.py:14
  118.3 23.7 %while.19 = (s32[]{:T(128)}, f32[256,512]{0,1:T(8,128)S(1)}, f32[8,256]{1,0:T(8,128)S(1)}, f32[15,8,256]{2,1,0:T(8,128)S(1)}, f32[15,256,512]{2,1,0:T(8,128)}, /*index=5*/s32[]{:T(128)}) while((s32[]{:T(128)}, f32[256,512]{0,1:T(8,128)S(1)}, f32[8,256]{1,0:T(8,128)S(1)}, f32[15,8,256]{2,1,0:T(8,128)S(1)}, f32[15,256,512]{2,1,0:T(8,128)}, ...), condition=%wide.region_3.4_spmd, body=%wide.region_2.3_spmd.sunk | while | flops 413698 | bytes 3743825 | solution.py:15
  118.3 1.1 constant_dynamic-slice_fusion.2
  119.9 1.1 constant_dynamic-slice_fusion.2
  121.5 1.1 constant_dynamic-slice_fusion.2
  123.1 1.1 constant_dynamic-slice_fusion.2
  124.7 1.1 constant_dynamic-slice_fusion.2
  126.2 1.1 constant_dynamic-slice_fusion.2
  127.8 1.1 constant_dynamic-slice_fusion.2
  129.4 1.1 constant_dynamic-slice_fusion.2
  131.0 1.1 constant_dynamic-slice_fusion.2
  132.5 1.1 constant_dynamic-slice_fusion.2
  134.1 1.1 constant_dynamic-slice_fusion.2
  135.7 1.1 constant_dynamic-slice_fusion.2
  137.3 1.1 constant_dynamic-slice_fusion.2
  138.8 1.1 constant_dynamic-slice_fusion.2
  140.4 1.1 constant_dynamic-slice_fusion.2
  142.9 2.3 %collective-permute-start = (bf16[15,512]{1,0:T(8,128)(2,1)S(1)}, bf16[15,512]{1,0:T(8,128)(2,1)S(1)}, u32[]{:S(2)}, u32[]{:S(2)}) collective-permute-start(bf16[15,512]{1,0:T(8,128)(2,1)S(1)} %get-tuple-element.99), channel_id=1, source_target_pairs={{0,1},{1,2},{2,3},{3,4},{4,5},{5,6},{6,7},{7,8},{8,9},{9,10},{10,1... | collective-permute-start | bytes 46088 | tf_op jit(solution)/shard_map/ppermute | solution.py:24
  145.2 2.0 %collective-permute-start.1 = (bf16[15,512]{1,0:T(8,128)(2,1)S(1)}, bf16[15,512]{1,0:T(8,128)(2,1)S(1)}, u32[]{:S(2)}, u32[]{:S(2)}) collective-permute-start(bf16[15,512]{1,0:T(8,128)(2,1)S(1)} %get-tuple-element.100), channel_id=1, source_target_pairs={{1,0},{2,1},{3,2},{4,3},{5,4},{6,5},{7,6},{8,7},{9,8},{10,9},{11,1... | collective-permute-start | bytes 46088 | tf_op jit(solution)/shard_map/ppermute | solution.py:27
  147.3 3.0 %collective-permute-done.1 = bf16[15,512]{1,0:T(8,128)(2,1)S(1)} collective-permute-done((bf16[15,512]{1,0:T(8,128)(2,1)S(1)}, bf16[15,512]{1,0:T(8,128)(2,1)S(1)}, u32[]{:S(2)}, u32[]{:S(2)}) %collective-permute-start.1) | collective-permute-done | bytes 15392 | tf_op jit(solution)/shard_map/ppermute | solution.py:27
  150.3 2.0 %fusion.16 = bf16[16,512]{1,0:T(8,128)(2,1)} fusion(f32[16,512]{1,0:T(8,128)S(1)} %get-tuple-element.104, bf16[512,512]{1,0:T(8,128)(2,1)} %param.25, f32[46,512]{1,0:T(8,128)S(1)} %maximum_convert_fusion, f32[512]{0:T(512)S(1)} %copy-done.6, f32[512]{0:T(512)S(1)} %copy-done.7, f32[512]{0:T(512)S(1)} %bitcast.130, f32[512]{0:T(512)S(1)} %bitcast.131, ...), kind=kOutput, calls=%fused_computation.26 | convolution fusion | flops 8962048 | bytes 1656832 | tf_op jit(solution)/shard_map/dot_general | solution.py:119
  (94 shorter events, 8.1 us)
Async XLA Ops:
  6.5 136.0 %copy-start = (bf16[512,1024]{1,0:T(8,128)(2,1)S(1)}, bf16[512,1024]{1,0:T(8,128)(2,1)}, u32[]{:S(2)}) copy-start(bf16[512,1024]{1,0:T(8,128)(2,1)} %param.21) | copy-start | bytes 3145732
  6.5 102.8 %all-gather.3.cloned.1.call-start = ((), (), s32[]{:S(2)}) async-start(), calls=%async_computation | async-start | bytes 8912896 | tf_op jit(solution)/shard_map/while/body/eval_jaxpr/all_gather | solution.py:12
  32.6 2.1 %copy-start.1 = (bf16[512,512]{1,0:T(8,128)(2,1)S(1)}, bf16[512,512]{1,0:T(8,128)(2,1)}, u32[]{:S(2)}) copy-start(bf16[512,512]{1,0:T(8,128)(2,1)} %param.17) | copy-start | bytes 1572868
  32.6 2.1 %copy-start.2 = (bf16[512,512]{1,0:T(8,128)(2,1)S(1)}, bf16[512,512]{1,0:T(8,128)(2,1)}, u32[]{:S(2)}) copy-start(bf16[512,512]{1,0:T(8,128)(2,1)} %param.19) | copy-start | bytes 1572868
  35.2 20.7 %copy-start.4 = (f32[31,512]{1,0:T(8,128)S(1)}, f32[31,512]{1,0:T(8,128)}, u32[]{:S(2)}) copy-start(f32[31,512]{1,0:T(8,128)} %param.22) | copy-start | bytes 190468
  118.2 23.7 %copy-start.3 = (bf16[512,512]{1,0:T(8,128)(2,1)S(1)}, bf16[512,512]{1,0:T(8,128)(2,1)}, u32[]{:S(2)}) copy-start(bf16[512,512]{1,0:T(8,128)(2,1)} %param.20) | copy-start | bytes 1572868
  118.2 23.7 %copy-start.5 = (bf16[16,512]{1,0:T(8,128)(2,1)S(1)}, bf16[16,512]{1,0:T(8,128)(2,1)}, u32[]{:S(2)}) copy-start(bf16[16,512]{1,0:T(8,128)(2,1)} %param.14) | copy-start | bytes 49156
  118.2 32.1 %copy-start.6 = (f32[512]{0:T(512)S(1)}, f32[512]{0:T(512)}, u32[]{:S(2)}) copy-start(f32[512]{0:T(512)} %param.24) | copy-start | bytes 6148
  118.2 32.1 %copy-start.7 = (f32[512]{0:T(512)S(1)}, f32[512]{0:T(512)}, u32[]{:S(2)}) copy-start(f32[512]{0:T(512)} %param.23) | copy-start | bytes 6148
  142.9 4.4 %collective-permute-start = (bf16[15,512]{1,0:T(8,128)(2,1)S(1)}, bf16[15,512]{1,0:T(8,128)(2,1)S(1)}, u32[]{:S(2)}, u32[]{:S(2)}) collective-permute-start(bf16[15,512]{1,0:T(8,128)(2,1)S(1)} %get-tuple-element.99), channel_id=1, source_target_pairs={{0,1},{1,2},{2,3},{3,4},{4,5},{5,6},{6,7},{7,8},{8,9},{9,10},{10,1... | collective-permute-start | bytes 46088 | tf_op jit(solution)/shard_map/ppermute | solution.py:24
  145.2 5.1 %collective-permute-start.1 = (bf16[15,512]{1,0:T(8,128)(2,1)S(1)}, bf16[15,512]{1,0:T(8,128)(2,1)S(1)}, u32[]{:S(2)}, u32[]{:S(2)}) collective-permute-start(bf16[15,512]{1,0:T(8,128)(2,1)S(1)} %get-tuple-element.100), channel_id=1, source_target_pairs={{1,0},{2,1},{3,2},{4,3},{5,4},{6,5},{7,6},{8,7},{9,8},{10,9},{11,1... | collective-permute-start | bytes 46088 | tf_op jit(solution)/shard_map/ppermute | solution.py:27
Sparse Core Ops, SparseCore 0:
  37.5 71.8 all-gather.2
where the time goes:
time: 161 us; the launch traced here: 159 us
  waiting for transfers between devices  56.4 us (35%)
  blocking collectives  42.4 us (26%)
  local copies, waits for them, and re-layouts  30.6 us (19%)
  between operations  13.6 us (8%)
  other arithmetic  6.08 us (4%)
  matrix products  5.08 us (3%)
  starting transfers between devices  4.33 us (3%)
    all_gather x1, waiting for transfers between devices, combined_all(): pieces = jax.tree.map(lambda part: lax.all_gather(part, axis), value)  53.4 us
    all_gather x1, blocking collectives, body(): gathered = lax.all_gather(query_rows, 'seq', axis=0, tiled=True)  23.9 us
    dynamic_slice x30, local copies, waits for them, and re-layouts, combined_all(): lax.scan(lambda so_far, section: (join(so_far, section), None), head, tail)  19.2 us
    all_gather x1, blocking collectives, combined_all(): pieces = jax.tree.map(lambda part: lax.all_gather(part, axis), value)  18.5 us
    slice x2, local copies, waits for them, and re-layouts, combined_all(): tail = jax.tree.map(lambda part: part[1:], pieces)  7.61 us
    add x15, other arithmetic, combine_partial(): return (out_first * share_first + out_second * share_second, joint)  3.24 us
  transfers between devices with their start and end apart: 3, of which 2 were waited for; matrix products, arithmetic and copies ran while one was open for 0% of the time, Pallas kernels for 0%

commit v1 on v0

v1 whole, which is shorter than its diff:
```python
import functools

import jax
import jax.numpy as jnp
from jax import lax
from jax.experimental import pallas as pl
from jax.experimental.pallas import tpu as pltpu
from jax.sharding import PartitionSpec as P

HEADS = 8
CORES = 2
MESH = pl.DeviceIdType.MESH
F32 = jnp.float32
BF16 = jnp.bfloat16


def dot(a, b):
    return jnp.dot(a, b, preferred_element_type=F32)


def layer_kernel(
    n,
    group,
    span_hbm,
    query_hbm,
    key_hbm,
    context_hbm,
    mask_hbm,
    value_w_hbm,
    out_w_hbm,
    expand_w_hbm,
    depth_hbm,
    scale_hbm,
    shift_hbm,
    project_w_hbm,
    out_ref,
    span,
    own_query,
    keys,
    context,
    mask,
    value_w,
    out_w,
    expand_w,
    depth,
    norm_scale,
    norm_shift,
    project_w,
    value_out,
    values,
    queries,
    partial_out,
    partials,
    spread,
    bias,
    gated,
    halo,
    padded,
    load_sem,
    query_send,
    query_recv,
    part_send,
    part_recv,
    pair_send,
    pair_recv,
    halo_send,
    halo_recv,
):
    me = lax.axis_index("seq")
    core = lax.rem(me, CORES)
    other = 1 - core
    pair = me - core + other
    rows, width = span.shape
    half = width // CORES
    frames = context.shape[0]
    heads = HEADS // CORES
    head_dim = width // HEADS
    block_rows = group * rows
    blocks = n // group
    lane_slot = 128 // heads

    barrier = pltpu.get_barrier_semaphore()

    def greet(step, carry):
        peer = lax.rem(me + step, n)
        pl.semaphore_signal(barrier, inc=1, device_id={"seq": peer}, device_id_type=MESH)
        return carry

    lax.fori_loop(1, n, greet, 0)

    def columns(index):
        return pl.ds(pl.multiple_of(index * half, half), half)

    loads = []

    def load(src, dst):
        copy = pltpu.make_async_copy(src, dst, load_sem.at[len(loads)])
        copy.start()
        loads.append(copy)
        return copy

    load_context = load(context_hbm, context)
    load_value_w = load(value_w_hbm, value_w)
    load_query = [load(query_hbm.at[:, i * half : (i + 1) * half], own_query.at[i]) for i in range(CORES)]
    load_mask = load(mask_hbm, mask.at[core])
    load_keys = load(key_hbm.at[:, columns(core)], keys.at[core])
    load_rest = [
        load(src, dst)
        for src, dst in (
            (span_hbm, span),
            (out_w_hbm, out_w),
            (expand_w_hbm, expand_w),
            (depth_hbm, depth),
            (scale_hbm, norm_scale),
            (shift_hbm, norm_shift),
            (project_w_hbm, project_w),
        )
    ]

    load_context.wait()
    load_value_w.wait()
    value_out[...] = dot(context[...], value_w[:, columns(other)]).astype(BF16)
    for copy in load_query:
        copy.wait()
    load_mask.wait()

    pl.semaphore_wait(barrier, n - 1)

    def remote(src, dst, send, recv, peer):
        return pltpu.make_async_remote_copy(
            src_ref=src,
            dst_ref=dst,
            send_sem=send,
            recv_sem=recv,
            device_id={"seq": peer},
            device_id_type=MESH,
        )

    def query_copy(peer, slot, sem_index):
        return remote(
            own_query.at[lax.rem(peer, CORES)],
            queries.at[slot],
            query_send.at[sem_index],
            query_recv.at[slot],
            peer,
        )

    key_copy = remote(
        key_hbm.at[:, columns(other)], keys.at[core], pair_send.at[0], pair_recv.at[0], pair
    )
    mask_copy = remote(mask.at[core], mask.at[core], pair_send.at[1], pair_recv.at[1], pair)
    value_copy = remote(value_out, values.at[core], pair_send.at[2], pair_recv.at[2], pair)
    key_copy.start()
    mask_copy.start()

    def send_query(step, carry):
        peer = lax.rem(me + step, n)
        query_copy(peer, me, peer).start()
        return carry

    lax.fori_loop(1, n, send_query, 0)
    value_copy.start()

    values[core] = dot(context[...], value_w[:, columns(core)]).astype(BF16)
    queries[me] = own_query[core]
    slot_row = lax.broadcasted_iota(jnp.int32, (128, 2 * half), 0)
    slot_col = lax.broadcasted_iota(jnp.int32, (128, 2 * half), 1)
    slot_head = lax.rem(slot_col, half) // head_dim * lane_slot
    shift_pick = jnp.logical_and(slot_col < half, slot_row == slot_head)
    total_pick = jnp.logical_and(
        slot_col >= half,
        jnp.logical_or(
            slot_row == slot_head + lane_slot // 2, slot_row == slot_head + lane_slot * 3 // 4
        ),
    )
    spread[...] = jnp.where(jnp.logical_or(shift_pick, total_pick), 1.0, 0.0).astype(BF16)

    load_keys.wait()
    remote(keys.at[other], keys.at[other], pair_send.at[0], pair_recv.at[0], pair).wait_recv()
    remote(mask.at[other], mask.at[other], pair_send.at[1], pair_recv.at[1], pair).wait_recv()
    for i in range(CORES):
        bias[:, i * frames : (i + 1) * frames] = jnp.where(mask[i] > 0, 0.0, -1e30)
    remote(values.at[other], values.at[other], pair_send.at[2], pair_recv.at[2], pair).wait_recv()

    head_lane = lax.broadcasted_iota(jnp.int32, (1, half), 1) // head_dim
    stat_lane = lax.broadcasted_iota(jnp.int32, (1, 128), 1)
    first_block = me // group
    heading = 1 - 2 * (2 * first_block // blocks)

    def attend(step, carry):
        block = lax.rem(first_block + heading * step + blocks, blocks)
        for i in range(group):
            source = block * group + i

            @pl.when(source != me)
            def _():
                query_copy(pair, source, source).wait_recv()

        query = queries[pl.ds(block * group, group)].reshape(block_rows, half)
        stacked = jnp.concatenate(
            [query * jnp.where(head_lane == h, head_dim**-0.5, 0.0).astype(BF16) for h in range(heads)],
            axis=0,
        )
        scores = (
            lax.dot_general(
                stacked,
                keys[...].reshape(CORES * frames, half),
                (((1,), (1,)), ((), ())),
                preferred_element_type=F32,
            )
            + bias[...]
        )
        shift = jnp.ceil(jnp.max(scores, axis=1, keepdims=True) * 0.25)
        shift = (shift.astype(BF16).astype(F32)) * 4.0
        weights = jnp.exp(scores - shift)
        total = jnp.sum(weights, axis=1, keepdims=True)
        numer = dot(weights.astype(BF16), values[...].reshape(CORES * frames, half))
        high = total.astype(BF16).astype(F32)
        low = total - high
        packed = jnp.zeros((block_rows, half), F32)
        stats = jnp.zeros((block_rows, 128), F32)
        for h in range(heads):
            part = slice(h * block_rows, (h + 1) * block_rows)
            packed = jnp.where(head_lane == h, numer[part], packed)
            begin = h * lane_slot
            stats = jnp.where(stat_lane >= begin, shift[part], stats)
            stats = jnp.where(stat_lane >= begin + lane_slot // 2, high[part], stats)
            stats = jnp.where(stat_lane >= begin + lane_slot * 3 // 4, low[part], stats)
        partial_out[pl.ds(block * group, group), :, :half] = packed.astype(BF16).reshape(
            group, rows, half
        )
        partial_out[pl.ds(block * group, group), :, half:] = stats.astype(BF16).reshape(
            group, rows, 128
        )
        for i in range(group):
            peer = block * group + i

            @pl.when(peer != me)
            def _():
                remote(
                    partial_out.at[peer], partials.at[me], part_send.at[peer], part_recv.at[me], peer
                ).start()

        return carry

    lax.fori_loop(0, blocks, attend, 0)
    partials[me] = partial_out[me]

    for copy in load_rest:
        copy.wait()

    def take_part(step, carry):
        peer = lax.rem(me + step, n)
        remote(
            partial_out.at[peer], partials.at[peer], part_send.at[peer], part_recv.at[peer], peer
        ).wait_recv()
        return carry

    lax.fori_loop(1, n, take_part, 0)

    chips = n // CORES
    stats = dot(partials[:, :, half:].reshape(n * rows, 128), spread[...])
    stats = stats.reshape(chips, CORES, rows, 2 * half)
    numers = partials[:, :, :half].astype(F32).reshape(chips, CORES, rows, half)
    shifts = stats[:, :, :, :half]
    shares = jnp.exp(shifts - jnp.max(shifts, axis=0, keepdims=True))
    attended = jnp.sum(shares * numers, axis=0) / jnp.sum(shares * stats[:, :, :, half:], axis=0)
    attended = jnp.concatenate([attended[i] for i in range(CORES)], axis=1).astype(BF16)

    wide = span[...].astype(F32) + dot(attended, out_w[...])
    mixed = wide.astype(BF16).astype(F32)
    centre = jnp.mean(mixed, axis=1, keepdims=True)
    deviation = mixed - centre
    variance = jnp.mean(deviation * deviation, axis=1, keepdims=True)
    normed = (deviation / jnp.sqrt(variance + 1e-05)).astype(BF16)
    expanded = dot(normed, expand_w[...])
    gated[...] = (expanded[:, :width] * jax.nn.sigmoid(expanded[:, width:])).astype(BF16)

    def halo_copy(side, peer):
        return remote(gated, halo.at[side], halo_send.at[side], halo_recv.at[side], peer)

    @pl.when(me < n - 1)
    def _():
        halo_copy(0, me + 1).start()

    @pl.when(me > 0)
    def _():
        halo_copy(1, me - 1).start()

    padded[rows : 2 * rows] = gated[...].astype(F32)

    @pl.when(me > 0)
    def _():
        halo_copy(0, me - 1).wait_recv()
        padded[:rows] = halo[0].astype(F32)

    @pl.when(me == 0)
    def _():
        padded[:rows] = jnp.zeros((rows, width), F32)

    @pl.when(me < n - 1)
    def _():
        halo_copy(1, me + 1).wait_recv()
        padded[2 * rows :] = halo[1].astype(F32)

    @pl.when(me == n - 1)
    def _():
        padded[2 * rows :] = jnp.zeros((rows, width), F32)

    taps = depth.shape[0]
    first = rows - taps // 2
    conv = jnp.zeros((rows, width), F32)
    for tap in range(taps):
        conv = conv + padded[first + tap : first + tap + rows] * depth[tap : tap + 1]
    normal = conv * norm_scale[...] + norm_shift[...]
    activated = (normal * jax.nn.sigmoid(normal)).astype(BF16)
    out_ref[...] = (mixed + dot(activated, project_w[...])).astype(BF16)

    def finish(step, carry):
        peer = lax.rem(me + step, n)
        query_copy(peer, me, peer).wait_send()
        remote(
            partial_out.at[peer], partials.at[me], part_send.at[peer], part_recv.at[me], peer
        ).wait_send()
        return carry

    lax.fori_loop(1, n, finish, 0)
    key_copy.wait_send()
    mask_copy.wait_send()
    value_copy.wait_send()

    @pl.when(me < n - 1)
    def _():
        halo_copy(0, me + 1).wait_send()

    @pl.when(me > 0)
    def _():
        halo_copy(1, me - 1).wait_send()


def body(
    n,
    span_frames,
    query_rows,
    key_rows,
    context_frames,
    key_mask,
    value_weight,
    out_weight,
    expand_weight,
    depth_weight,
    norm_scale,
    norm_shift,
    project_weight,
):
    rows, width = span_frames.shape
    frames = key_rows.shape[0]
    half = width // CORES
    group = max(1, min(n, 64 // rows))
    vmem = pltpu.VMEM
    dma = pltpu.SemaphoreType.DMA
    args = (
        span_frames,
        query_rows,
        key_rows,
        context_frames,
        key_mask.reshape(1, frames),
        value_weight,
        out_weight,
        expand_weight,
        depth_weight,
        norm_scale.reshape(1, width),
        norm_shift.reshape(1, width),
        project_weight,
    )
    return pl.pallas_call(
        functools.partial(layer_kernel, n, group),
        out_shape=jax.ShapeDtypeStruct((rows, width), BF16),
        in_specs=[pl.BlockSpec(memory_space=pl.ANY)] * len(args),
        out_specs=pl.BlockSpec(memory_space=pltpu.VMEM),
        scratch_shapes=[
            vmem((rows, width), BF16),
            vmem((CORES, rows, half), BF16),
            vmem((CORES, frames, half), BF16),
            vmem((frames, width), BF16),
            vmem((CORES, 1, frames), jnp.int32),
            vmem(value_weight.shape, BF16),
            vmem(out_weight.shape, BF16),
            vmem(expand_weight.shape, BF16),
            vmem(depth_weight.shape, F32),
            vmem((1, width), F32),
            vmem((1, width), F32),
            vmem(project_weight.shape, BF16),
            vmem((frames, half), BF16),
            vmem((CORES, frames, half), BF16),
            vmem((n, rows, half), BF16),
            vmem((n, rows, half + 128), BF16),
            vmem((n, rows, half + 128), BF16),
            vmem((128, 2 * half), BF16),
            vmem((1, CORES * frames), F32),
            vmem((rows, width), BF16),
            vmem((2, rows, width), BF16),
            vmem((3 * rows, width), F32),
            dma((16,)),
            dma((n,)),
            dma((n,)),
            dma((n,)),
            dma((n,)),
            dma((3,)),
            dma((3,)),
            dma((2,)),
            dma((2,)),
        ],
        compiler_params=pltpu.CompilerParams(collective_id=0, has_side_effects=True),
    )(*args)


def solution(mesh):
    rows = P(("groups", "seq"), None)
    in_specs = (rows, rows, rows, rows, P(("groups", "seq"))) + (P(),) * 7
    return jax.shard_map(
        functools.partial(body, mesh.shape["seq"]),
        mesh=mesh,
        in_specs=in_specs,
        out_specs=rows,
        check_vma=False,
    )
```

time: 161 us -> 24.1 us (0.15); the launches traced: 159 us -> 23.9 us
  waiting for transfers between devices: 56.4 us -> 0 us
  blocking collectives: 42.4 us -> 0 us
  local copies, waits for them, and re-layouts: 30.6 us -> 1.32 us
  Pallas kernels: 0 us -> 22.6 us
  between operations: 13.6 us -> 0.01 us
  other arithmetic: 6.08 us -> 0 us
  matrix products: 5.08 us -> 0 us
  starting transfers between devices: 4.33 us -> 0 us
    all_gather x1 -> x0, waiting for transfers between devices: 53.4 us -> none  [combined_all(): pieces = jax.tree.map(lambda part: lax.all_gather(part, axis), value)]
    all_gather x2 -> x0, blocking collectives: 42.4 us -> none  [the longest x1 23.9 us: body(): gathered = lax.all_gather(query_rows, 'seq', axis=0, tiled=True)]
    pallas_call x0 -> x1, Pallas kernels: none -> 22.6 us  [body(): pl.pallas_call(functools.partial(layer_kernel, n, group), out_shape=jax.S...]
    dynamic_slice x30 -> x0, local copies, waits for them, and re-layouts: 19.2 us -> none  [combined_all(): lax.scan(lambda so_far, section: (join(so_far, section), None), head, tail)]
    slice x6 -> x0, local copies, waits for them, and re-layouts: 7.67 us -> none  [the longest x2 7.61 us: combined_all(): tail = jax.tree.map(lambda part: part[1:], pieces)]
    dot_general x6 -> x0, matrix products: 5.08 us -> none  [the longest x1 1.99 us: body(): jnp.dot(activated, project_weight, preferred_element_type=jnp.float32)]
    ppermute x2 -> x0, starting transfers between devices: 4.32 us -> none  [the longest x1 2.33 us: with_halo(): lax.ppermute(lax.slice_in_dim(block, block.shape[dim] - width, None, axis...]
    add x16 -> x0, other arithmetic: 3.24 us -> none  [the longest x15 3.24 us: combine_partial(): return (out_first * share_first + out_second * share_second, joint)]
  transfers between devices with their start and end apart: 3 -> 0, of which waited for: 2 -> 0; matrix products, arithmetic and copies ran while one was open for 0% -> 0% of each run, Pallas kernels for 0% -> 0%
where the time goes in v1:
time: 24.1 us; the launch traced here: 23.9 us
  Pallas kernels  22.6 us (94%)
  local copies, waits for them, and re-layouts  1.32 us (5%)
    pallas_call x1, Pallas kernels, body(): pl.pallas_call(functools.partial(layer_kernel, n, group), out_shape=jax.S...  22.6 us
    unnamed x1, local copies, waits for them, and re-layouts  1.32 us

profile of v1, /device:TPU:1, one launch (start us, length us, event | category | flops | bytes accessed | tf_op | source)
XLA Modules:
  0.0 23.9 jit_solution(11652331871547664567)
XLA Ops:
  0.0 22.6 %shard_map.118 = bf16[16,512]{1,0:T(8,128)(2,1)} custom-call(bf16[16,512]{1,0:T(8,128)(2,1)} %span_hbm.1, bf16[16,512]{1,0:T(8,128)(2,1)} %query_hbm.1, bf16[512,512]{1,0:T(8,128)(2,1)} %key_hbm.1, bf16[512,512]{1,0:T(8,128)(2,1)} %context_hbm.1, s32[1,512]{1,0:T(1,128)} %bitcast.3, bf16[512,512]{1,0:T(8,128)(2,1)} %value_w_hbm.1, ...), custom_call_target="tpu_custom_call" | custom-call | tf_op jit(solution)/shard_map/pallas_call | solution.py:376
  22.6 1.3 %copy.14 = bf16[16,512]{1,0:T(8,128)(2,1)} copy(bf16[16,512]{1,0:T(8,128)(2,1)} %shard_map.118) | data formatting | bytes 32768

commit v2 on v1

--- a/solution.py
+++ b/solution.py
@@ -124,45 +124,7 @@
         copy.wait()
     load_mask.wait()
 
-    pl.semaphore_wait(barrier, n - 1)
-
-    def remote(src, dst, send, recv, peer):
-        return pltpu.make_async_remote_copy(
-            src_ref=src,
-            dst_ref=dst,
-            send_sem=send,
-            recv_sem=recv,
-            device_id={"seq": peer},
-            device_id_type=MESH,
-        )
-
-    def query_copy(peer, slot, sem_index):
-        return remote(
-            own_query.at[lax.rem(peer, CORES)],
-            queries.at[slot],
-            query_send.at[sem_index],
-            query_recv.at[slot],
-            peer,
-        )
-
-    key_copy = remote(
-        key_hbm.at[:, columns(other)], keys.at[core], pair_send.at[0], pair_recv.at[0], pair
-    )
-    mask_copy = remote(mask.at[core], mask.at[core], pair_send.at[1], pair_recv.at[1], pair)
-    value_copy = remote(value_out, values.at[core], pair_send.at[2], pair_recv.at[2], pair)
-    key_copy.start()
-    mask_copy.start()
-
-    def send_query(step, carry):
-        peer = lax.rem(me + step, n)
-        query_copy(peer, me, peer).start()
-        return carry
-
-    lax.fori_loop(1, n, send_query, 0)
-    value_copy.start()
-
     values[core] = dot(context[...], value_w[:, columns(core)]).astype(BF16)
-    queries[me] = own_query[core]
     slot_row = lax.broadcasted_iota(jnp.int32, (128, 2 * half), 0)
     slot_col = lax.broadcasted_iota(jnp.int32, (128, 2 * half), 1)
     slot_head = lax.rem(slot_col, half) // head_dim * lane_slot
@@ -175,6 +137,44 @@
     )
     spread[...] = jnp.where(jnp.logical_or(shift_pick, total_pick), 1.0, 0.0).astype(BF16)
 
+    pl.semaphore_wait(barrier, n - 1)
+
+    def remote(src, dst, send, recv, peer):
+        return pltpu.make_async_remote_copy(
+            src_ref=src,
+            dst_ref=dst,
+            send_sem=send,
+            recv_sem=recv,
+            device_id={"seq": peer},
+            device_id_type=MESH,
+        )
+
+    def query_copy(peer, slot, sem_index):
+        return remote(
+            own_query.at[lax.rem(peer, CORES)],
+            queries.at[slot],
+            query_send.at[sem_index],
+            query_recv.at[slot],
+            peer,
+        )
+
+    key_copy = remote(
+        key_hbm.at[:, columns(other)], keys.at[core], pair_send.at[0], pair_recv.at[0], pair
+    )
+    mask_copy = remote(mask.at[core], mask.at[core], pair_send.at[1], pair_recv.at[1], pair)
+    value_copy = remote(value_out, values.at[core], pair_send.at[2], pair_recv.at[2], pair)
+    key_copy.start()
+    mask_copy.start()
+
+    def send_query(step, carry):
+        peer = lax.rem(me + step, n)
+        query_copy(peer, me, peer).start()
+        return carry
+
+    lax.fori_loop(1, n, send_query, 0)
+    value_copy.start()
+
+    queries[me] = own_query[core]
     load_keys.wait()
     remote(keys.at[other], keys.at[other], pair_send.at[0], pair_recv.at[0], pair).wait_recv()
     remote(mask.at[other], mask.at[other], pair_send.at[1], pair_recv.at[1], pair).wait_recv()
@@ -375,7 +375,7 @@
     )
     return pl.pallas_call(
         functools.partial(layer_kernel, n, group),
-        out_shape=jax.ShapeDtypeStruct((rows, width), BF16),
+        out_shape=pltpu.VMEM((rows, width), BF16),
         in_specs=[pl.BlockSpec(memory_space=pl.ANY)] * len(args),
         out_specs=pl.BlockSpec(memory_space=pltpu.VMEM),
         scratch_shapes=[

time: 24.1 us -> 22.9 us (0.950)
  local copies, waits for them, and re-layouts: 1.32 us -> 0.61 us
  Pallas kernels: 22.6 us -> 22.1 us
    unnamed x1, local copies, waits for them, and re-layouts: 1.32 us -> 0.61 us
    pallas_call x1, Pallas kernels: 22.6 us -> 22.1 us  [body(): pl.pallas_call(functools.partial(layer_kernel, n, group), out_shape=pltpu...]
where the time goes in v2:
time: 22.9 us; the launch traced here: 22.8 us
  Pallas kernels  22.1 us (97%)
  local copies, waits for them, and re-layouts  0.61 us (3%)
    pallas_call x1, Pallas kernels, body(): pl.pallas_call(functools.partial(layer_kernel, n, group), out_shape=pltpu...  22.1 us
    unnamed x1, local copies, waits for them, and re-layouts  0.61 us

profile of v2, /device:TPU:1, one launch (start us, length us, event | category | flops | bytes accessed | tf_op | source)
XLA Modules:
  0.0 22.8 jit_solution(7725032870220142566)
XLA Ops:
  0.0 22.1 %shard_map.118 = bf16[16,512]{1,0:T(8,128)(2,1)S(1)} custom-call(bf16[16,512]{1,0:T(8,128)(2,1)} %span_hbm.1, bf16[16,512]{1,0:T(8,128)(2,1)} %query_hbm.1, bf16[512,512]{1,0:T(8,128)(2,1)} %key_hbm.1, bf16[512,512]{1,0:T(8,128)(2,1)} %context_hbm.1, s32[1,512]{1,0:T(1,128)} %bitcast.3, bf16[512,512]{1,0:T(8,128)(2,1)} %value_w_hbm.1, ...), custom_call_target="tpu_custom_call" | custom-call | tf_op jit(solution)/shard_map/pallas_call | solution.py:376
  22.1 0.6 %copy.14 = bf16[16,512]{1,0:T(8,128)(2,1)} copy(bf16[16,512]{1,0:T(8,128)(2,1)S(1)} %shard_map.118) | data formatting | bytes 32768

commit v3 on v2

--- a/solution.py
+++ b/solution.py
@@ -51,6 +51,8 @@
     queries,
     partial_out,
     partials,
+    stat_out,
+    stat_in,
     spread,
     bias,
     gated,
@@ -61,6 +63,8 @@
     query_recv,
     part_send,
     part_recv,
+    stat_send,
+    stat_recv,
     pair_send,
     pair_recv,
     halo_send,
@@ -77,7 +81,6 @@
     head_dim = width // HEADS
     block_rows = group * rows
     blocks = n // group
-    lane_slot = 128 // heads
 
     barrier = pltpu.get_barrier_semaphore()
 
@@ -125,17 +128,17 @@
     load_mask.wait()
 
     values[core] = dot(context[...], value_w[:, columns(core)]).astype(BF16)
-    slot_row = lax.broadcasted_iota(jnp.int32, (128, 2 * half), 0)
-    slot_col = lax.broadcasted_iota(jnp.int32, (128, 2 * half), 1)
-    slot_head = lax.rem(slot_col, half) // head_dim * lane_slot
-    shift_pick = jnp.logical_and(slot_col < half, slot_row == slot_head)
-    total_pick = jnp.logical_and(
-        slot_col >= half,
-        jnp.logical_or(
-            slot_row == slot_head + lane_slot // 2, slot_row == slot_head + lane_slot * 3 // 4
-        ),
+    fields = 2 * heads
+    stat_width = stat_out.shape[-1]
+    slot = lax.rem(lax.broadcasted_iota(jnp.int32, (stat_width, 2 * half), 0), fields)
+    target = lax.broadcasted_iota(jnp.int32, (stat_width, 2 * half), 1)
+    wanted = lax.rem(target, half) // head_dim * 2 + target // half
+    spread[...] = jnp.where(slot == wanted, 1.0, 0.0).astype(BF16)
+    field = lax.rem(lax.broadcasted_iota(jnp.int32, (1, stat_width), 1), fields)
+    own_row = (
+        lax.broadcasted_iota(jnp.int32, (1, rows, stat_width), 2) // fields
+        == lax.broadcasted_iota(jnp.int32, (1, rows, stat_width), 1)
     )
-    spread[...] = jnp.where(jnp.logical_or(shift_pick, total_pick), 1.0, 0.0).astype(BF16)
 
     pl.semaphore_wait(barrier, n - 1)
 
@@ -158,6 +161,16 @@
             peer,
         )
 
+    def part_copies(peer, place):
+        return (
+            remote(
+                stat_out.at[peer], stat_in.at[place], stat_send.at[peer], stat_recv.at[place], peer
+            ),
+            remote(
+                partial_out.at[peer], partials.at[place], part_send.at[peer], part_recv.at[place], peer
+            ),
+        )
+
     key_copy = remote(
         key_hbm.at[:, columns(other)], keys.at[core], pair_send.at[0], pair_recv.at[0], pair
     )
@@ -183,7 +196,6 @@
     remote(values.at[other], values.at[other], pair_send.at[2], pair_recv.at[2], pair).wait_recv()
 
     head_lane = lax.broadcasted_iota(jnp.int32, (1, half), 1) // head_dim
-    stat_lane = lax.broadcasted_iota(jnp.int32, (1, 128), 1)
     first_block = me // group
     heading = 1 - 2 * (2 * first_block // blocks)
 
@@ -215,53 +227,48 @@
         weights = jnp.exp(scores - shift)
         total = jnp.sum(weights, axis=1, keepdims=True)
         numer = dot(weights.astype(BF16), values[...].reshape(CORES * frames, half))
-        high = total.astype(BF16).astype(F32)
-        low = total - high
         packed = jnp.zeros((block_rows, half), F32)
-        stats = jnp.zeros((block_rows, 128), F32)
+        stats = jnp.zeros((block_rows, stat_width), F32)
         for h in range(heads):
             part = slice(h * block_rows, (h + 1) * block_rows)
             packed = jnp.where(head_lane == h, numer[part], packed)
-            begin = h * lane_slot
-            stats = jnp.where(stat_lane >= begin, shift[part], stats)
-            stats = jnp.where(stat_lane >= begin + lane_slot // 2, high[part], stats)
-            stats = jnp.where(stat_lane >= begin + lane_slot * 3 // 4, low[part], stats)
-        partial_out[pl.ds(block * group, group), :, :half] = packed.astype(BF16).reshape(
-            group, rows, half
-        )
-        partial_out[pl.ds(block * group, group), :, half:] = stats.astype(BF16).reshape(
-            group, rows, 128
-        )
+            stats = jnp.where(field == 2 * h, shift[part], stats)
+            stats = jnp.where(field == 2 * h + 1, total[part], stats)
+        stats = jnp.where(own_row, stats.reshape(group, rows, stat_width), 0.0)
+        stat_out[pl.ds(block * group, group)] = jnp.sum(stats, axis=1, keepdims=True)
+        partial_out[pl.ds(block * group, group)] = packed.astype(BF16).reshape(group, rows, half)
         for i in range(group):
             peer = block * group + i
 
             @pl.when(peer != me)
             def _():
-                remote(
-                    partial_out.at[peer], partials.at[me], part_send.at[peer], part_recv.at[me], peer
-                ).start()
+                for copy in part_copies(peer, me):
+                    copy.start()
 
         return carry
 
     lax.fori_loop(0, blocks, attend, 0)
     partials[me] = partial_out[me]
+    stat_in[me] = stat_out[me]
 
     for copy in load_rest:
         copy.wait()
 
     def take_part(step, carry):
         peer = lax.rem(me + step, n)
-        remote(
-            partial_out.at[peer], partials.at[peer], part_send.at[peer], part_recv.at[peer], peer
-        ).wait_recv()
+        for copy in part_copies(peer, peer):
+            copy.wait_recv()
         return carry
 
     lax.fori_loop(1, n, take_part, 0)
 
     chips = n // CORES
-    stats = dot(partials[:, :, half:].reshape(n * rows, 128), spread[...])
+    stats = jnp.where(own_row, stat_in[...], 0.0).reshape(n * rows, stat_width)
+    high = stats.astype(BF16)
+    low = (stats - high.astype(F32)).astype(BF16)
+    stats = dot(high, spread[...]) + dot(low, spread[...])
     stats = stats.reshape(chips, CORES, rows, 2 * half)
-    numers = partials[:, :, :half].astype(F32).reshape(chips, CORES, rows, half)
+    numers = partials[...].astype(F32).reshape(chips, CORES, rows, half)
     shifts = stats[:, :, :, :half]
     shares = jnp.exp(shifts - jnp.max(shifts, axis=0, keepdims=True))
     attended = jnp.sum(shares * numers, axis=0) / jnp.sum(shares * stats[:, :, :, half:], axis=0)
@@ -319,9 +326,8 @@
     def finish(step, carry):
         peer = lax.rem(me + step, n)
         query_copy(peer, me, peer).wait_send()
-        remote(
-            partial_out.at[peer], partials.at[me], part_send.at[peer], part_recv.at[me], peer
-        ).wait_send()
+        for copy in part_copies(peer, me):
+            copy.wait_send()
         return carry
 
     lax.fori_loop(1, n, finish, 0)
@@ -357,6 +363,7 @@
     frames = key_rows.shape[0]
     half = width // CORES
     group = max(1, min(n, 64 // rows))
+    stat_width = rows * 2 * (HEADS // CORES)
     vmem = pltpu.VMEM
     dma = pltpu.SemaphoreType.DMA
     args = (
@@ -394,14 +401,18 @@
             vmem((frames, half), BF16),
             vmem((CORES, frames, half), BF16),
             vmem((n, rows, half), BF16),
-            vmem((n, rows, half + 128), BF16),
-            vmem((n, rows, half + 128), BF16),
-            vmem((128, 2 * half), BF16),
+            vmem((n, rows, half), BF16),
+            vmem((n, rows, half), BF16),
+            vmem((n, 1, stat_width), F32),
+            vmem((n, 1, stat_width), F32),
+            vmem((stat_width, 2 * half), BF16),
             vmem((1, CORES * frames), F32),
             vmem((rows, width), BF16),
             vmem((2, rows, width), BF16),
             vmem((3 * rows, width), F32),
             dma((16,)),
+            dma((n,)),
+            dma((n,)),
             dma((n,)),
             dma((n,)),
             dma((n,)),

time: 22.9 us -> 22.6 us (0.987)
  Pallas kernels: 22.1 us -> 21.8 us
    pallas_call x1, Pallas kernels: 22.1 us -> 21.8 us  [body(): pl.pallas_call(functools.partial(layer_kernel, n, group), out_shape=pltpu...]
where the time goes in v3:
time: 22.6 us; the launch traced here: 22.5 us
  Pallas kernels  21.8 us (96%)
  local copies, waits for them, and re-layouts  0.61 us (3%)
    pallas_call x1, Pallas kernels, body(): pl.pallas_call(functools.partial(layer_kernel, n, group), out_shape=pltpu...  21.8 us
    unnamed x1, local copies, waits for them, and re-layouts  0.61 us

profile of v3, /device:TPU:1, one launch (start us, length us, event | category | flops | bytes accessed | tf_op | source)
XLA Modules:
  0.0 22.5 jit_solution(251363220629400924)
XLA Ops:
  0.0 21.8 %shard_map.118 = bf16[16,512]{1,0:T(8,128)(2,1)S(1)} custom-call(bf16[16,512]{1,0:T(8,128)(2,1)} %span_hbm.1, bf16[16,512]{1,0:T(8,128)(2,1)} %query_hbm.1, bf16[512,512]{1,0:T(8,128)(2,1)} %key_hbm.1, bf16[512,512]{1,0:T(8,128)(2,1)} %context_hbm.1, s32[1,512]{1,0:T(1,128)} %bitcast.3, bf16[512,512]{1,0:T(8,128)(2,1)} %value_w_hbm.1, ...), custom_call_target="tpu_custom_call" | custom-call | tf_op jit(solution)/shard_map/pallas_call | solution.py:383
  21.8 0.6 %copy.14 = bf16[16,512]{1,0:T(8,128)(2,1)} copy(bf16[16,512]{1,0:T(8,128)(2,1)S(1)} %shard_map.118) | data formatting | bytes 32768

commit v4 on v3

--- a/solution.py
+++ b/solution.py
@@ -81,6 +81,7 @@
     head_dim = width // HEADS
     block_rows = group * rows
     blocks = n // group
+    unroll = n <= 32
 
     barrier = pltpu.get_barrier_semaphore()
 
@@ -89,7 +90,7 @@
         pl.semaphore_signal(barrier, inc=1, device_id={"seq": peer}, device_id_type=MESH)
         return carry
 
-    lax.fori_loop(1, n, greet, 0)
+    lax.fori_loop(1, n, greet, 0, unroll=unroll)
 
     def columns(index):
         return pl.ds(pl.multiple_of(index * half, half), half)
@@ -179,12 +180,20 @@
     key_copy.start()
     mask_copy.start()
 
+    first_block = me // group
+    heading = 1 - 2 * (2 * first_block // blocks)
+
     def send_query(step, carry):
-        peer = lax.rem(me + step, n)
-        query_copy(peer, me, peer).start()
+        spot = step
+        peer = lax.rem(first_block + heading * (spot // group) + blocks, blocks) * group + lax.rem(me + lax.rem(spot, group), group)
+
+        @pl.when(peer != me)
+        def _():
+            query_copy(peer, me, peer).start()
+
         return carry
 
-    lax.fori_loop(1, n, send_query, 0)
+    lax.fori_loop(0, n, send_query, 0, unroll=unroll)
     value_copy.start()
 
     queries[me] = own_query[core]
@@ -196,8 +205,6 @@
     remote(values.at[other], values.at[other], pair_send.at[2], pair_recv.at[2], pair).wait_recv()
 
     head_lane = lax.broadcasted_iota(jnp.int32, (1, half), 1) // head_dim
-    first_block = me // group
-    heading = 1 - 2 * (2 * first_block // blocks)
 
     def attend(step, carry):
         block = lax.rem(first_block + heading * step + blocks, blocks)
@@ -247,7 +254,7 @@
 
         return carry
 
-    lax.fori_loop(0, blocks, attend, 0)
+    lax.fori_loop(0, blocks, attend, 0, unroll=unroll)
     partials[me] = partial_out[me]
     stat_in[me] = stat_out[me]
 
@@ -260,7 +267,7 @@
             copy.wait_recv()
         return carry
 
-    lax.fori_loop(1, n, take_part, 0)
+    lax.fori_loop(1, n, take_part, 0, unroll=unroll)
 
     chips = n // CORES
     stats = jnp.where(own_row, stat_in[...], 0.0).reshape(n * rows, stat_width)
@@ -330,7 +337,7 @@
             copy.wait_send()
         return carry
 
-    lax.fori_loop(1, n, finish, 0)
+    lax.fori_loop(1, n, finish, 0, unroll=unroll)
     key_copy.wait_send()
     mask_copy.wait_send()
     value_copy.wait_send()

time: 22.6 us -> 21.7 us (0.960)
  Pallas kernels: 21.8 us -> 21 us
    pallas_call x1, Pallas kernels: 21.8 us -> 21 us  [body(): pl.pallas_call(functools.partial(layer_kernel, n, group), out_shape=pltpu...]
where the time goes in v4:
time: 21.7 us; the launch traced here: 21.6 us
  Pallas kernels  21 us (97%)
  local copies, waits for them, and re-layouts  0.61 us (3%)
    pallas_call x1, Pallas kernels, body(): pl.pallas_call(functools.partial(layer_kernel, n, group), out_shape=pltpu...  21 us
    unnamed x1, local copies, waits for them, and re-layouts  0.61 us

profile of v4, /device:TPU:1, one launch (start us, length us, event | category | flops | bytes accessed | tf_op | source)
XLA Modules:
  0.0 21.6 jit_solution(13314512164649933123)
XLA Ops:
  0.0 21.0 %shard_map.118 = bf16[16,512]{1,0:T(8,128)(2,1)S(1)} custom-call(bf16[16,512]{1,0:T(8,128)(2,1)} %span_hbm.1, bf16[16,512]{1,0:T(8,128)(2,1)} %query_hbm.1, bf16[512,512]{1,0:T(8,128)(2,1)} %key_hbm.1, bf16[512,512]{1,0:T(8,128)(2,1)} %context_hbm.1, s32[1,512]{1,0:T(1,128)} %bitcast.3, bf16[512,512]{1,0:T(8,128)(2,1)} %value_w_hbm.1, ...), custom_call_target="tpu_custom_call" | custom-call | tf_op jit(solution)/shard_map/pallas_call | solution.py:390
  21.0 0.6 %copy.14 = bf16[16,512]{1,0:T(8,128)(2,1)} copy(bf16[16,512]{1,0:T(8,128)(2,1)S(1)} %shard_map.118) | data formatting | bytes 32768

commit v5 on v4

--- a/solution.py
+++ b/solution.py
@@ -202,7 +202,6 @@
     remote(mask.at[other], mask.at[other], pair_send.at[1], pair_recv.at[1], pair).wait_recv()
     for i in range(CORES):
         bias[:, i * frames : (i + 1) * frames] = jnp.where(mask[i] > 0, 0.0, -1e30)
-    remote(values.at[other], values.at[other], pair_send.at[2], pair_recv.at[2], pair).wait_recv()
 
     head_lane = lax.broadcasted_iota(jnp.int32, (1, half), 1) // head_dim
 
@@ -233,6 +232,13 @@
         shift = (shift.astype(BF16).astype(F32)) * 4.0
         weights = jnp.exp(scores - shift)
         total = jnp.sum(weights, axis=1, keepdims=True)
+
+        @pl.when(step == 0)
+        def _():
+            remote(
+                values.at[other], values.at[other], pair_send.at[2], pair_recv.at[2], pair
+            ).wait_recv()
+
         numer = dot(weights.astype(BF16), values[...].reshape(CORES * frames, half))
         packed = jnp.zeros((block_rows, half), F32)
         stats = jnp.zeros((block_rows, stat_width), F32)

time: 21.7 us -> 21.9 us (level)
  no operation moved by 1% of the time
where the time goes in v5:
time: 21.9 us; the launch traced here: 21.8 us
  Pallas kernels  21.2 us (97%)
  local copies, waits for them, and re-layouts  0.61 us (3%)
    pallas_call x1, Pallas kernels, body(): pl.pallas_call(functools.partial(layer_kernel, n, group), out_shape=pltpu...  21.2 us
    unnamed x1, local copies, waits for them, and re-layouts  0.61 us

profile of v5, /device:TPU:1, one launch (start us, length us, event | category | flops | bytes accessed | tf_op | source)
XLA Modules:
  0.0 21.8 jit_solution(16103081486982085766)
XLA Ops:
  0.0 21.2 %shard_map.118 = bf16[16,512]{1,0:T(8,128)(2,1)S(1)} custom-call(bf16[16,512]{1,0:T(8,128)(2,1)} %span_hbm.1, bf16[16,512]{1,0:T(8,128)(2,1)} %query_hbm.1, bf16[512,512]{1,0:T(8,128)(2,1)} %key_hbm.1, bf16[512,512]{1,0:T(8,128)(2,1)} %context_hbm.1, s32[1,512]{1,0:T(1,128)} %bitcast.3, bf16[512,512]{1,0:T(8,128)(2,1)} %value_w_hbm.1, ...), custom_call_target="tpu_custom_call" | custom-call | tf_op jit(solution)/shard_map/pallas_call | solution.py:396
  21.2 0.6 %copy.14 = bf16[16,512]{1,0:T(8,128)(2,1)} copy(bf16[16,512]{1,0:T(8,128)(2,1)S(1)} %shard_map.118) | data formatting | bytes 32768
